TPU v7x, 32 devices: a whole 2x2x4 slice. The times are simulated.
32 devices in a mesh: groups: 2 (over y), sample: 2 (over core), space: 8 (over z, x).
Axes of the slice: x: 2, y: 2, z: 4, core: 2. Of those that a mesh axis runs over, the one named last changes fastest.
Arguments:
- features: bfloat16 [4, 16, 16, 16, 128], P(('groups', 'sample'), 'space'), parts along dimension 0, may hold values from -6 to 6
- w_fine: bfloat16 [27, 128, 128], replicated, may hold values from -0.109375 to 0.109375
- w_down: bfloat16 [8, 128, 256], replicated, may hold values from -0.1875 to 0.1875
- mixing: bfloat16 [8, 8], replicated, may hold values from -2 to 2
- cotangent: bfloat16 [4, 8, 16384], P(('groups', 'sample'), None, 'space'), parts along dimension 0, may hold values from -6 to 6
Outputs:
- bottleneck: bfloat16 [4, 8, 16384], P(('groups', 'sample'), None, 'space'), parts along dimension 0
- feature_grad: bfloat16 [4, 16, 16, 16, 128], P(('groups', 'sample'), 'space'), parts along dimension 0
- fine_grad: float32 [884736], P(('groups', 'space')), parts along dimension 0
- down_grad: float32 [524288], P(('groups', 'space')), parts along dimension 0
- mixing_grad: float32 [16, 8], P(('groups', 'space')), parts along dimension 0
There are 2 independent parts, one for each index of `groups`. A program takes and returns all parts, laid end to end along the dimension named above; an argument that names none is the same for every part. Nothing has to cross between parts.
All inputs are finite; a program needn't handle non-finite values.
Results may differ from a plain program's by a relative error of at most 0.0065.
Values may be sent and summed in bfloat16 or wider, within the bound.
A program may use at most 64 MiB of HBM per device.

v0:
```python
import jax
import jax.numpy as jnp
from jax import lax
from jax.sharding import PartitionSpec as P


def with_halo(array, sides, width):
    for axis, dim in sides:
        devices, length = (lax.axis_size(axis), array.shape[dim])
        up = [(i, (i + 1) % devices) for i in range(devices - 1)]
        down = [(j, i) for i, j in up]
        last = lax.slice_in_dim(array, length - width, length, axis=dim)
        initial = lax.slice_in_dim(array, 0, width, axis=dim)
        before = lax.ppermute(last, axis, up)
        after = lax.ppermute(initial, axis, down)
        array = jnp.concatenate([before, array, after], axis=dim)
    return array


def forward_conv(padded, weight, count):
    extent_x = padded.shape[2] - 2
    extent_z = padded.shape[3] - 2
    channels = padded.shape[4]
    total = None
    for shift_y in range(3):
        for shift_x in range(3):
            pieces = [
                padded[
                    :,
                    shift_y : shift_y + count,
                    shift_x : shift_x + extent_x,
                    shift_z : shift_z + extent_z,
                    :,
                ]
                for shift_z in range(3)
            ]
            stacked = jnp.concatenate(pieces, axis=-1).reshape(-1, 3 * channels)
            first = shift_y * 9 + shift_x * 3
            kernel = weight[first : first + 3].reshape(3 * channels, weight.shape[2])
            term = jnp.dot(stacked, kernel, preferred_element_type=jnp.float32)
            total = term if total is None else total + term
    return total.reshape(padded.shape[0], count, extent_x, extent_z, weight.shape[2])


def transposed_conv(padded, weight, count):
    extent_x = padded.shape[2] - 2
    extent_z = padded.shape[3] - 2
    channels = padded.shape[4]
    total = None
    for shift_y in range(3):
        for shift_x in range(3):
            pieces = [
                padded[
                    :,
                    2 - shift_y : 2 - shift_y + count,
                    2 - shift_x : 2 - shift_x + extent_x,
                    2 - shift_z : 2 - shift_z + extent_z,
                    :,
                ]
                for shift_z in range(3)
            ]
            stacked = jnp.concatenate(pieces, axis=-1).reshape(-1, 3 * channels)
            first = shift_y * 9 + shift_x * 3
            kernel = jnp.swapaxes(weight[first : first + 3], 1, 2).reshape(
                3 * channels, weight.shape[1]
            )
            term = jnp.dot(stacked, kernel, preferred_element_type=jnp.float32)
            total = term if total is None else total + term
    return total.reshape(padded.shape[0], count, extent_x, extent_z, weight.shape[1])


def weight_terms(padded, grad, count):
    extent_x = padded.shape[2] - 2
    extent_z = padded.shape[3] - 2
    channels = padded.shape[4]
    flat_grad = grad.reshape(-1, grad.shape[4])
    blocks = []
    for shift_y in range(3):
        for shift_x in range(3):
            pieces = [
                padded[
                    :,
                    shift_y : shift_y + count,
                    shift_x : shift_x + extent_x,
                    shift_z : shift_z + extent_z,
                    :,
                ]
                for shift_z in range(3)
            ]
            stacked = jnp.concatenate(pieces, axis=-1).reshape(-1, 3 * channels)
            blocks.append(
                lax.dot_general(
                    stacked, flat_grad, (((0,), (0,)), ((), ())), preferred_element_type=jnp.float32
                )
            )
    return jnp.concatenate(blocks, axis=0).reshape(-1)


def fold_taps(hidden):
    batch, rows_here, extent_x, extent_z, channels = hidden.shape
    shaped = hidden.reshape(batch, rows_here // 2, 2, extent_x // 2, 2, extent_z // 2, 2, channels)
    return shaped.transpose(0, 1, 3, 5, 2, 4, 6, 7).reshape(-1, 8 * channels)


def unfold_taps(values, batch, rows_here, extent_x, extent_z, channels):
    shaped = values.reshape(batch, rows_here // 2, extent_x // 2, extent_z // 2, 2, 2, 2, channels)
    return shaped.transpose(0, 1, 4, 2, 5, 3, 6, 7).reshape(
        batch, rows_here, extent_x, extent_z, channels
    )


def silu_slope(value):
    sigma = jax.nn.sigmoid(value)
    return sigma * (1.0 + value * (1.0 - sigma))


def local(features, w_fine, w_down, mixing, cotangent):
    batch, rows_here, extent_x, extent_z, channels = features.shape
    coarse_ch = w_down.shape[2]
    rimmed = with_halo(features, (("space", 1),), 1)
    xpadded = jnp.pad(rimmed, ((0, 0), (0, 0), (1, 1), (1, 1), (0, 0)))
    act = forward_conv(xpadded, w_fine, rows_here)
    hidden = (features.astype(jnp.float32) + jax.nn.silu(act)).astype(jnp.bfloat16)
    folded = fold_taps(hidden)
    down_matrix = w_down.reshape(8 * channels, coarse_ch)
    coarse = jnp.dot(folded, down_matrix, preferred_element_type=jnp.float32).astype(jnp.bfloat16)
    coarse = coarse.reshape(batch, rows_here // 2, -1)
    columns = lax.all_to_all(coarse, "space", split_axis=2, concat_axis=1, tiled=True)
    mixed = jnp.stack([jnp.dot(mixing, columns[0], preferred_element_type=jnp.float32)])
    bottleneck = (columns.astype(jnp.float32) + jax.nn.silu(mixed)).astype(jnp.bfloat16)
    cot = cotangent.astype(jnp.float32)
    mixed_grad = (cot * silu_slope(mixed)).astype(jnp.bfloat16)
    term = lax.dot_general(
        mixed_grad[0], columns[0], (((1,), (1,)), ((), ())), preferred_element_type=jnp.float32
    )
    spread_list = [
        lax.dot_general(
            mixing, mixed_grad[0], (((0,), (0,)), ((), ())), preferred_element_type=jnp.float32
        )
    ]
    column_grad = (cot + jnp.stack(spread_list)).astype(jnp.bfloat16)
    coarse_grad = lax.all_to_all(column_grad, "space", split_axis=1, concat_axis=2, tiled=True)
    flat_coarse = coarse_grad.reshape(-1, coarse_ch)
    down_terms = lax.dot_general(
        folded, flat_coarse, (((0,), (0,)), ((), ())), preferred_element_type=jnp.float32
    ).reshape(-1)
    hidden_grad = unfold_taps(
        jnp.dot(flat_coarse, down_matrix.T, preferred_element_type=jnp.float32),
        batch,
        rows_here,
        extent_x,
        extent_z,
        channels,
    )
    act_grad = (hidden_grad * silu_slope(act)).astype(jnp.bfloat16)
    grad_rim = with_halo(act_grad, (("space", 1),), 1)
    gpadded = jnp.pad(grad_rim, ((0, 0), (0, 0), (1, 1), (1, 1), (0, 0)))
    spread = transposed_conv(gpadded, w_fine, rows_here)
    feature_grad = (hidden_grad + spread).astype(jnp.bfloat16)
    fine_terms = weight_terms(xpadded, act_grad, rows_here)
    scale = float(
        batch * lax.axis_size("sample") * rows_here * lax.axis_size("space") * extent_x * extent_z
    ) ** (-0.5)
    shares = (
        lax.psum_scatter(fine_terms, "space", scatter_dimension=0, tiled=True),
        lax.psum_scatter(down_terms, "space", scatter_dimension=0, tiled=True),
        lax.psum_scatter(term, "space", scatter_dimension=0, tiled=True),
    )
    totals = lax.psum((shares[0], shares[1], shares[2]), "sample")
    return (bottleneck, feature_grad, totals[0] * scale, totals[1] * scale, totals[2] * scale)


def solution(mesh):
    placed = (
        P(("groups", "sample"), "space", None, None, None),
        P(),
        P(),
        P(),
        P(("groups", "sample"), None, "space"),
    )
    return jax.shard_map(
        local,
        mesh=mesh,
        in_specs=placed,
        out_specs=(
            P(("groups", "sample"), None, "space"),
            P(("groups", "sample"), "space", None, None, None),
            P(("groups", "space")),
            P(("groups", "space")),
            P(("groups", "space"), None),
        ),
        check_vma=False,
    )
```

profile of v0, /device:TPU:0, one launch (start us, length us, event | category | flops | bytes accessed | tf_op | source)
XLA Modules:
  0.0 502.1 jit_solution(10094833240650439102)
XLA Ops:
  7.2 1.0 fusion.49
  8.1 4.9 collective-permute-start
  13.0 1.3 collective-permute-start.1
  14.3 1.5 slice_bitcast_fusion
  15.9 3.3 collective-permute-done.1
  24.1 10.2 %reshape.457 = bf16[1,1,16384]{1,0,2:T(2,128)(2,1)} reshape(bf16[64,256]{1,0:T(8,128)(2,1)S(1)} %convolution_convert_fusion) | data formatting | bytes 65536 | tf_op jit(solution)/shard_map/reshape | solution.py:127
  34.8 123.6 %reduce.5 = bf16[16384]{0:T(1024)(128)(2,1)S(1)} reduce(bf16[16384,1,1]{2,1,0:T(2,128)(2,1)} %bitcast.254, bf16[]{:T(256)} %broadcast.164), dimensions={1,2}, to_apply=%bitcast.187.reduce_sub_computation | reduce | bytes 65538
  158.4 0.6 reshape.465
  159.0 5.8 %all-to-all-start = ((bf16[8,2,1024]{2,1,0:T(2,128)(2,1)}), bf16[8,2,1024]{2,1,0:T(2,128)(2,1)S(1)}, u32[]{:S(2)}, u32[]{:S(2)}) async-start(bf16[8,2,1024]{2,1,0:T(2,128)(2,1)} %reshape.465), calls=%async_computation | async-start | bytes 65536 | tf_op jit(solution)/shard_map/all_to_all | solution.py:128
  164.8 0.6 dynamic-slice
  167.8 3.6 all-to-all-done
  171.5 10.2 %reshape.466 = bf16[16384,1,1]{2,1,0:T(2,128)(2,1)} reshape(bf16[8,2,1024]{2,1,0:T(2,128)(2,1)S(1)} %all-to-all-done) | data formatting | bytes 65536
  181.7 122.9 %bitcast_reduce_fusion = bf16[16384]{0:T(1024)(128)(2,1)S(1)} fusion(bf16[16384,1,1]{2,1,0:T(2,128)(2,1)} %reshape.466), kind=kLoop, calls=%fused_computation.128 | loop fusion | bytes 65536 | tf_op jit(solution)/shard_map/all_to_all | solution.py:128
  305.2 0.8 reduce.6
  306.1 0.6 reshape.467
  306.7 18.2 %all-reduce.4 = f32[8,8]{1,0:T(8,128)S(1)} all-reduce(f32[8,8]{1,0:T(8,128)S(1)} %fusion.39), channel_id=4, replica_groups=mesh['groups'=2,'sample'=2,'space'=8] {'space'}, use_global_device_ids=true, to_apply=%region_4.5.clone | all-reduce | flops 64 | bytes 512
  324.9 0.6 constant_dynamic-slice_fusion
  325.5 3.3 all-to-all-start.1
  328.9 2.5 psum.23
  331.4 0.6 fusion.42
  332.5 2.9 all-to-all-done.1
  343.3 2.4 collective-permute-start.2
  345.7 1.5 collective-permute-start.3
  347.7 1.6 copy.90
  349.3 2.5 collective-permute-done.3
  355.2 116.0 %all-reduce.10.cloned.1.call-done = (f32[442368]{0:T(1024)}, f32[262144]{0:T(1024)}) async-done(((f32[442368]{0:T(1024)}, f32[262144]{0:T(1024)}), (f32[442368]{0:T(1024)}, f32[262144]{0:T(1024)})) %all-reduce.10.cloned.1.call-update) | async-done | bytes 2818064
  471.3 1.6 dynamic-slice.1
  472.9 1.6 dynamic-slice.3
  474.8 0.7 add_convert_fusion
  475.5 16.6 %all-reduce.12.cloned.1.call-done = (f32[55296]{0:T(1024)}, f32[32768]{0:T(1024)}) async-done(((f32[55296]{0:T(1024)}, f32[32768]{0:T(1024)}), (f32[55296]{0:T(1024)}, f32[32768]{0:T(1024)})) %all-reduce.12.cloned.1.call-update) | async-done | bytes 352272 | tf_op jit(solution)/shard_map/psum | solution.py:169
  492.1 1.6 broadcast_multiply_fusion
  493.7 1.6 broadcast_multiply_fusion.1
  (159 shorter events, 19.1 us)
Async XLA Ops:
  7.2 16.8 %copy-start = (bf16[8,128,256]{2,1,0:T(8,128)(2,1)S(1)}, bf16[8,128,256]{2,1,0:T(8,128)(2,1)}, u32[]{:S(2)}) copy-start(bf16[8,128,256]{2,1,0:T(8,128)(2,1)} %param.7) | copy-start | bytes 1572868
  7.2 12.0 %copy-start.1 = (bf16[1,2,16,16,128]{4,3,2,1,0:T(8,128)(2,1)S(1)}, bf16[1,2,16,16,128]{4,3,2,1,0:T(8,128)(2,1)}, u32[]{:S(2)}) copy-start(bf16[1,2,16,16,128]{4,3,2,1,0:T(8,128)(2,1)} %param.5) | copy-start | bytes 393220
  8.1 7.7 %collective-permute-start = (bf16[1,1,16,16,128]{4,3,2,1,0:T(8,128)(2,1)S(1)}, bf16[1,1,16,16,128]{4,3,2,1,0:T(8,128)(2,1)S(1)}, u32[]{:S(2)}, u32[]{:S(2)}) collective-permute-start(bf16[1,1,16,16,128]{4,3,2,1,0:T(8,128)(2,1)S(1)} %get-tuple-element.82), channel_id=1, source_target_pairs={{0,1},{1,2},{2,3},{3,4},{4,5},{5,6},{6,7},{8,9},{9,10},{10,11},{11... | collective-permute-start | bytes 196616 | tf_op jit(solution)/shard_map/ppermute | solution.py:14
  13.0 6.2 %collective-permute-start.1 = (bf16[1,1,16,16,128]{4,3,2,1,0:T(8,128)(2,1)S(1)}, bf16[1,1,16,16,128]{4,3,2,1,0:T(8,128)(2,1)S(1)}, u32[]{:S(2)}, u32[]{:S(2)}) collective-permute-start(bf16[1,1,16,16,128]{4,3,2,1,0:T(8,128)(2,1)S(1)} %get-tuple-element.83), channel_id=1, source_target_pairs={{1,0},{2,1},{3,2},{4,3},{5,4},{6,5},{7,6},{9,8},{10,9},{11,10},{12... | collective-permute-start | bytes 196616 | tf_op jit(solution)/shard_map/ppermute | solution.py:15
  19.8 1.7 copy-start.21
  19.8 1.7 copy-start.23
  19.8 1.7 copy-start.25
  19.8 1.7 copy-start.27
  19.8 1.7 copy-start.29
  19.8 1.7 copy-start.31
  19.8 2.7 copy-start.5
  19.8 2.7 copy-start.7
  19.9 2.7 copy-start.9
  19.9 2.7 copy-start.11
  19.9 2.7 copy-start.13
  19.9 2.7 copy-start.15
  20.0 1.2 copy-start.35
  20.4 1.5 copy-start.3
  34.8 130.0 %copy-start.39 = (u32[32]{0:T(128)S(1)}, u32[32]{0:T(128)}, u32[]{:S(2)}) copy-start(u32[32]{0:T(128)} %constant.22) | copy-start | bytes 388
  159.0 12.4 %all-to-all-start = ((bf16[8,2,1024]{2,1,0:T(2,128)(2,1)}), bf16[8,2,1024]{2,1,0:T(2,128)(2,1)S(1)}, u32[]{:S(2)}, u32[]{:S(2)}) async-start(bf16[8,2,1024]{2,1,0:T(2,128)(2,1)} %reshape.465), calls=%async_computation | async-start | bytes 65536 | tf_op jit(solution)/shard_map/all_to_all | solution.py:128
  181.7 123.0 %copy-start.37 = (bf16[1,8,2048]{2,1,0:T(8,128)(2,1)S(1)}, bf16[1,8,2048]{2,1,0:T(8,128)(2,1)}, u32[]{:S(2)}) copy-start(bf16[1,8,2048]{2,1,0:T(8,128)(2,1)} %param.9) | copy-start | bytes 98308
  181.7 123.0 %copy-start.38 = (bf16[8,8]{1,0:T(8,128)(2,1)S(1)}, bf16[8,8]{1,0:T(8,128)(2,1)}, u32[]{:S(2)}) copy-start(bf16[8,8]{1,0:T(8,128)(2,1)} %param.8) | copy-start | bytes 388
  304.6 31.5 %copy-start.34 = (bf16[1,2,16,16,128]{4,3,2,1,0:T(8,128)(2,1)S(1)}, bf16[1,2,16,16,128]{4,3,2,1,0:T(8,128)(2,1)}, u32[]{:S(2)}) copy-start(bf16[1,2,16,16,128]{4,3,2,1,0:T(8,128)(2,1)} %copy-done.33) | copy-start | bytes 393220
  304.6 31.5 %copy-start.36 = (bf16[1,2,16,16,128]{4,3,2,1,0:T(8,128)(2,1)S(1)}, bf16[1,2,16,16,128]{4,3,2,1,0:T(8,128)(2,1)}, u32[]{:S(2)}) copy-start(bf16[1,2,16,16,128]{4,3,2,1,0:T(8,128)(2,1)} %copy-done.35) | copy-start | bytes 393220
  325.5 10.0 %all-to-all-start.1 = ((bf16[8,2,1024]{2,1,0:T(2,128)(2,1)}), bf16[8,2,1024]{2,1,0:T(2,128)(2,1)S(1)}, u32[]{:S(2)}, u32[]{:S(2)}) async-start(bf16[8,2,1024]{2,1,0:T(2,128)(2,1)} %reshape.467), calls=%async_computation.1 | async-start | bytes 65536 | tf_op jit(solution)/shard_map/all_to_all | solution.py:142
  328.8 142.4 %all-reduce.10.cloned.1.call-start = ((), (), s32[]{:S(2)}) async-start(), calls=%async_computation.2 | async-start | bytes 5636096
  337.0 1.0 copy-start.32
  338.0 1.0 copy-start.26
  343.0 6.2 %copy-start.2 = (f32[3456,128]{1,0:T(8,128)}, f32[3456,128]{1,0:T(8,128)S(1)}, u32[]{:S(2)}) copy-start(f32[3456,128]{1,0:T(8,128)S(1)} %fusion.2) | copy-start | bytes 5308420
  343.3 6.0 %collective-permute-start.2 = (bf16[1,1,16,16,128]{4,3,2,1,0:T(8,128)(2,1)S(1)}, bf16[1,1,16,16,128]{4,3,2,1,0:T(8,128)(2,1)S(1)}, u32[]{:S(2)}, u32[]{:S(2)}) collective-permute-start(bf16[1,1,16,16,128]{4,3,2,1,0:T(8,128)(2,1)S(1)} %get-tuple-element.77), channel_id=1, source_target_pairs={{0,1},{1,2},{2,3},{3,4},{4,5},{5,6},{6,7},{8,9},{9,10},{10,11},{11... | collective-permute-start | bytes 196616 | tf_op jit(solution)/shard_map/ppermute | solution.py:14
  345.7 6.2 %collective-permute-start.3 = (bf16[1,1,16,16,128]{4,3,2,1,0:T(8,128)(2,1)S(1)}, bf16[1,1,16,16,128]{4,3,2,1,0:T(8,128)(2,1)S(1)}, u32[]{:S(2)}, u32[]{:S(2)}) collective-permute-start(bf16[1,1,16,16,128]{4,3,2,1,0:T(8,128)(2,1)S(1)} %get-tuple-element.78), channel_id=1, source_target_pairs={{1,0},{2,1},{3,2},{4,3},{5,4},{6,5},{7,6},{9,8},{10,9},{11,10},{12... | collective-permute-start | bytes 196616 | tf_op jit(solution)/shard_map/ppermute | solution.py:15
  349.3 142.8 %all-reduce.12.cloned.1.call-start = ((), (), s32[]{:S(2)}) async-start(), calls=%async_computation.3 | async-start | bytes 704512 | tf_op jit(solution)/shard_map/psum | solution.py:169
  (16 other events, 14.6 us)
Sparse Core Ops, SparseCore 0:
  349.4 121.8 all-reduce.9
  474.6 17.4 all-reduce.11
where the time goes:
time: 503 us; the launch traced here: 502 us
  local copies, waits for them, and re-layouts  161 us (32%)
  waiting for transfers between devices  145 us (29%)
  other arithmetic  131 us (26%)
  blocking collectives  20.7 us (4%)
  starting transfers between devices  19.2 us (4%)
  between operations  16.2 us (3%)
  matrix products  8.79 us (2%)
    unnamed x2, other arithmetic  124 us
    all_to_all x2, local copies, waits for them, and re-layouts, local(): lax.all_to_all(coarse, 'space', split_axis=2, concat_axis=1, tiled=True)  123 us
    unnamed x3, waiting for transfers between devices  116 us
    unnamed x90, local copies, waits for them, and re-layouts  22.8 us
    unnamed x1, blocking collectives  18.2 us
    psum x1, waiting for transfers between devices, local(): totals = lax.psum((shares[0], shares[1], shares[2]), 'sample')  16.6 us
    reshape x1, local copies, waits for them, and re-layouts, local(): coarse = coarse.reshape(batch, rows_here // 2, -1)  10.2 us
  transfers between devices with their start and end apart: 8, of which 6 were waited for; matrix products, arithmetic and copies ran while one was open for 2% of the time, Pallas kernels for 0%

commit v1 on v0

--- a/solution.py
+++ b/solution.py
@@ -1,7 +1,405 @@
+import functools
+
 import jax
 import jax.numpy as jnp
 from jax import lax
+from jax.experimental import pallas as pl
+from jax.experimental.pallas import tpu as pltpu
 from jax.sharding import PartitionSpec as P
+
+MESH = pl.DeviceIdType.MESH
+F32 = jnp.float32
+BF16 = jnp.bfloat16
+CONTRACT_LAST = (((1,), (1,)), ((), ()))
+CONTRACT_FIRST = (((0,), (0,)), ((), ()))
+
+
+def fused_body(
+    cfg,
+    features, w_fine, w_down, mixing, cotangent,
+    bottleneck, feature_grad, fine_out, down_out, mixing_out,
+    x_halo, g_halo, grad16, pad, x3, g3, xt, act, hid, folded, folded_t,
+    stage, fwd_send, fwd_recv, back_send, back_recv, hid_grad,
+    fine16, fine_peer, fine_send, fine_recv,
+    down16, down_peer, down_send, down_recv,
+    mix_send, mix_recv, mix_total, mix_peer,
+    fine_half, fine_half_peer, down_half, down_half_peer,
+    halo_s, halo_r, fwd_s, fwd_r, back_s, back_r, mix_s, mix_r,
+    ghalo_s, ghalo_r, peer_s, peer_r, dpeer_s, dpeer_r,
+    fine_s, fine_r, down_s, down_r, last_s, last_r,
+):
+    n, ex, ez, ch, cc, scale = cfg
+    plane = ex * ez
+    hx, hz = ex // 2, ez // 2
+    lanes = 128
+    rows = hx * hz * cc // lanes // n
+    halves = cc // lanes
+    fine_rows = 27 * ch // n
+    part = fine_send.shape[1]
+    fine_step = fine_rows - part
+    fine_mine = fine_rows // 2
+    down_rows = 8 * ch // n
+    down_part = down_rows // 2
+    me = lax.axis_index("space")
+    core = lax.axis_index("sample")
+    other = 1 - core
+
+    def to_space(src, dst, send, recv, who):
+        return pltpu.make_async_remote_copy(
+            src_ref=src, dst_ref=dst, send_sem=send, recv_sem=recv,
+            device_id={"space": who}, device_id_type=MESH,
+        )
+
+    def to_peer(src, dst, send, recv):
+        return pltpu.make_async_remote_copy(
+            src_ref=src, dst_ref=dst, send_sem=send, recv_sem=recv,
+            device_id={"sample": other}, device_id_type=MESH,
+        )
+
+    has_prev, has_next = me > 0, me < n - 1
+
+    @pl.when(me == 0)
+    def _():
+        x_halo[0] = jnp.zeros(x_halo.shape[1:], BF16)
+        g_halo[0] = jnp.zeros(g_halo.shape[1:], BF16)
+
+    @pl.when(me == n - 1)
+    def _():
+        x_halo[1] = jnp.zeros(x_halo.shape[1:], BF16)
+        g_halo[1] = jnp.zeros(g_halo.shape[1:], BF16)
+
+    barrier = pltpu.get_barrier_semaphore()
+    for k in range(1, n):
+        pl.semaphore_signal(
+            barrier, inc=1, device_id={"space": lax.rem(me + k, n)}, device_id_type=MESH
+        )
+    pl.semaphore_signal(barrier, inc=1, device_id={"sample": other}, device_id_type=MESH)
+    pl.semaphore_wait(barrier, n)
+
+    def halo_copies(first, last, halo, send, recv):
+        down = to_space(first, halo.at[1], send.at[0], recv.at[1], me - 1)
+        up = to_space(last, halo.at[0], send.at[1], recv.at[0], me + 1)
+        return down, up
+
+    def start_halo(copies):
+        pl.when(has_prev)(copies[0].start)
+        pl.when(has_next)(copies[1].start)
+
+    def wait_halo(copies):
+        def with_prev():
+            copies[0].wait_send()
+            copies[1].wait_recv()
+
+        def with_next():
+            copies[1].wait_send()
+            copies[0].wait_recv()
+
+        pl.when(has_prev)(with_prev)
+        pl.when(has_next)(with_next)
+
+    x_copies = halo_copies(features.at[0, 0], features.at[0, 1], x_halo, halo_s, halo_r)
+    start_halo(x_copies)
+
+    pad[:, :, 0:8, :] = jnp.zeros((2, ex, 8, ch), F32)
+    pad[:, :, 8 + ez : 16 + ez, :] = jnp.zeros((2, ex, 8, ch), F32)
+    for rim in (0, ex + 1):
+        x3[:, rim] = jnp.zeros((4, ez, 3 * ch), BF16)
+        g3[:, rim] = jnp.zeros((4, ez, 3 * ch), BF16)
+
+    def spread_rows(dest, index, row, slot):
+        pad[slot, :, 8 : 8 + ez, :] = row.astype(F32)
+        dest[index, 1 : 1 + ex, :, 0:ch] = pad[slot, :, 7 : 7 + ez, :].astype(BF16)
+        dest[index, 1 : 1 + ex, :, ch : 2 * ch] = row
+        dest[index, 1 : 1 + ex, :, 2 * ch : 3 * ch] = pad[slot, :, 9 : 9 + ez, :].astype(BF16)
+
+    def window(source, index, shift):
+        return source[index, shift : shift + ex].reshape(plane, 3 * ch)
+
+    def taps(sy, sx):
+        first = sy * 9 + sx * 3
+        return w_fine[first : first + 3].reshape(3 * ch, ch)
+
+    def mm(a, b):
+        return jnp.dot(a, b, preferred_element_type=F32)
+
+    spread_rows(x3, 1, features[0, 0], 0)
+    spread_rows(x3, 2, features[0, 1], 1)
+    total = None
+    for sx in range(3):
+        term = mm(window(x3, 1, sx), jnp.concatenate([taps(1, sx), taps(0, sx)], axis=1))
+        total = term if total is None else total + term
+        total = total + mm(
+            window(x3, 2, sx), jnp.concatenate([taps(2, sx), taps(1, sx)], axis=1)
+        )
+    act[...] = total
+    wait_halo(x_copies)
+    spread_rows(x3, 0, x_halo[0], 0)
+    spread_rows(x3, 3, x_halo[1], 1)
+    for side in range(2):
+        total = act[:, side * ch : (side + 1) * ch]
+        for sx in range(3):
+            total = total + mm(window(x3, 3 * side, sx), taps(2 * side, sx))
+        act[:, side * ch : (side + 1) * ch] = total
+        value = features[0, side].reshape(plane, ch).astype(F32) + total * jax.nn.sigmoid(total)
+        hid[side] = value.astype(BF16).astype(F32).reshape(hx, 2, ez, ch)
+
+    for t in range(8):
+        i, j, k = t // 4, t // 2 % 2, t % 2
+        piece = hid[i, :, j, pl.ds(k, hz, stride=2), :].reshape(hx * hz, ch)
+        folded[:, t * ch : (t + 1) * ch] = piece.astype(BF16)
+    coarse = mm(folded[...], w_down[...].reshape(8 * ch, cc)).astype(BF16).astype(F32)
+    for h in range(halves):
+        stage[pl.ds(h, hx * hz, stride=halves), :] = coarse[:, h * lanes : (h + 1) * lanes]
+    fwd_send[...] = stage[...].astype(BF16).reshape(n, rows, lanes)
+
+    def exchange(src_of, slots, send, recv):
+        out = []
+        for k in range(1, n):
+            who = lax.rem(me + k, n)
+            copy = to_space(src_of(who), slots.at[me], send.at[k - 1], recv.at[k - 1], who)
+            copy.start()
+            out.append(copy)
+        return out
+
+    coarse_copies = exchange(lambda who: fwd_send.at[who], fwd_recv, fwd_s, fwd_r)
+    fwd_recv[me] = fwd_send[me]
+
+    folded_t[...] = folded[...].T
+    for sx in range(3):
+        for j in range(4):
+            xt[sx, :, j * plane : (j + 1) * plane] = window(x3, j, sx).T
+
+    for copy in coarse_copies:
+        copy.wait()
+    stage[...] = fwd_recv[...].reshape(n * rows, lanes).astype(F32)
+    columns = jnp.concatenate([stage[pl.ds(r, n, stride=rows), :] for r in range(rows)], axis=1)
+    columns16 = columns.astype(BF16)
+    mix = mixing[...]
+    mixed = mm(mix, columns16)
+    sigma = jax.nn.sigmoid(mixed)
+    bottleneck[0] = (columns + mixed * sigma).astype(BF16)
+    cot = cotangent[0].astype(F32)
+    mixed_grad = (cot * (sigma * (1.0 + mixed * (1.0 - sigma)))).astype(BF16)
+    spread = lax.dot_general(mix, mixed_grad, CONTRACT_FIRST, preferred_element_type=F32)
+    column_grad = cot + spread
+    for r in range(rows):
+        stage[pl.ds(r, n, stride=rows), :] = column_grad[:, r * lanes : (r + 1) * lanes]
+    back_send[...] = stage[...].astype(BF16).reshape(n, rows, lanes)
+    back_copies = exchange(lambda who: back_send.at[who], back_recv, back_s, back_r)
+    back_recv[me] = back_send[me]
+    term = lax.dot_general(mixed_grad, columns16, CONTRACT_LAST, preferred_element_type=F32)
+    mix_send[...] = jnp.zeros(mix_send.shape, F32)
+    mix_send[:, 0:n] = term
+    mix_copies = exchange(lambda who: mix_send, mix_recv, mix_s, mix_r)
+    mix_recv[me] = mix_send[...]
+
+    for copy in back_copies:
+        copy.wait()
+    stage[...] = back_recv[...].reshape(n * rows, lanes).astype(F32)
+    flat = jnp.concatenate(
+        [stage[pl.ds(h, hx * hz, stride=halves), :] for h in range(halves)], axis=1
+    ).astype(BF16)
+
+    for t in range(8):
+        i, j, k = t // 4, t // 2 % 2, t % 2
+        piece = lax.dot_general(flat, w_down[t], CONTRACT_LAST, preferred_element_type=F32)
+        hid_grad[i, :, j, pl.ds(k, hz, stride=2), :] = piece.reshape(hx, hz, ch)
+    for side in range(2):
+        value = act[:, side * ch : (side + 1) * ch]
+        sig = jax.nn.sigmoid(value)
+        slope = sig * (1.0 + value * (1.0 - sig))
+        grad = hid_grad[side].reshape(plane, ch) * slope
+        grad16[side] = grad.astype(BF16).reshape(ex, ez, ch)
+    g_copies = halo_copies(grad16.at[0], grad16.at[1], g_halo, ghalo_s, ghalo_r)
+    start_halo(g_copies)
+
+    down16[...] = mm(folded_t[...], flat).astype(BF16).reshape(n, down_rows, cc)
+    dpeer = to_peer(
+        down16.at[:, pl.ds(pl.multiple_of(other * down_part, 16), down_part), :],
+        down_peer, dpeer_s, dpeer_r,
+    )
+    dpeer.start()
+
+    flat_grad = grad16[...].reshape(2 * plane, ch)
+    peer_copies = []
+    done = 0
+    down_copies = []
+    for t in range(9):
+        sy, sx = t // 3, t % 3
+        block = mm(xt[sx, :, sy * plane : (sy + 2) * plane], flat_grad)
+        fine16[t * 3 * ch : (t + 1) * 3 * ch, :] = block.astype(BF16)
+        while done < n and (done + 1) * fine_rows <= (t + 1) * 3 * ch:
+            start = pl.multiple_of(done * fine_rows + other * fine_step, 16)
+            copy = to_peer(
+                fine16.at[pl.ds(start, part), :], fine_peer.at[done],
+                peer_s.at[done], peer_r.at[done],
+            )
+            copy.start()
+            peer_copies.append(copy)
+            done += 1
+        if t == 3:
+            dpeer.wait()
+            mine = down16[:, pl.ds(pl.multiple_of(core * down_part, 16), down_part), :]
+            down_send[...] = (mine.astype(F32) + down_peer[...].astype(F32)).astype(BF16)
+            down_copies = exchange(lambda who: down_send.at[who], down_recv, down_s, down_r)
+            down_recv[me] = down_send[me]
+
+    fine_copies = []
+    for copy in peer_copies:
+        copy.wait()
+    for k in range(1, n + 1):
+        who = lax.rem(me + k, n)
+        start = pl.multiple_of(who * fine_rows + core * fine_step, 16)
+        mine = fine16[pl.ds(start, part), :].astype(F32) + fine_peer[who].astype(F32)
+        if k < n:
+            fine_send[who] = mine.astype(BF16)
+            copy = to_space(
+                fine_send.at[who], fine_recv.at[me], fine_s.at[k - 1], fine_r.at[k - 1], who
+            )
+            copy.start()
+            fine_copies.append(copy)
+        else:
+            fine_recv[me] = mine.astype(BF16)
+
+    def turned(i, sx):
+        first = i * 9 + sx * 3
+        return jnp.concatenate([w_fine[first + 2 - m] for m in range(3)], axis=1)
+
+    def mt(a, b):
+        return lax.dot_general(a, b, CONTRACT_LAST, preferred_element_type=F32)
+
+    spread_rows(g3, 1, grad16[0], 0)
+    spread_rows(g3, 2, grad16[1], 1)
+    total = None
+    for sx in range(3):
+        term = mt(window(g3, 1, 2 - sx), jnp.concatenate([turned(1, sx), turned(2, sx)], axis=0))
+        total = term if total is None else total + term
+        total = total + mt(
+            window(g3, 2, 2 - sx), jnp.concatenate([turned(0, sx), turned(1, sx)], axis=0)
+        )
+    act[...] = total
+    wait_halo(g_copies)
+    spread_rows(g3, 0, g_halo[0], 0)
+    spread_rows(g3, 3, g_halo[1], 1)
+    for side in range(2):
+        total = act[:, side * ch : (side + 1) * ch] + hid_grad[side].reshape(plane, ch)
+        for sx in range(3):
+            total = total + mt(window(g3, 3 * side, 2 - sx), turned(2 - 2 * side, sx))
+        feature_grad[0, side] = total.astype(BF16).reshape(ex, ez, ch)
+
+    for copy in mix_copies:
+        copy.wait()
+    mix_total[...] = sum(mix_recv[s] for s in range(n)) * scale
+    mix_swap = to_peer(mix_total, mix_peer, last_s.at[0], last_r.at[0])
+    mix_swap.start()
+
+    for copy in down_copies:
+        copy.wait()
+    value = sum(down_recv[s].astype(F32) for s in range(n)) * scale
+    for h in range(halves):
+        down_half[pl.ds(h, down_part, stride=halves), :] = value[:, h * lanes : (h + 1) * lanes]
+    down_swap = to_peer(down_half, down_half_peer, last_s.at[1], last_r.at[1])
+    down_swap.start()
+
+    for copy in fine_copies:
+        copy.wait()
+    value = sum(fine_recv[s].astype(F32) for s in range(n)) * scale
+    begin = fine_mine - fine_step
+    fine_half[...] = jnp.where(core == 0, value[0:fine_mine], value[begin : begin + fine_mine])
+    fine_swap = to_peer(fine_half, fine_half_peer, last_s.at[2], last_r.at[2])
+    fine_swap.start()
+
+    down_len = down_part * halves
+    fine_out[pl.ds(pl.multiple_of(core * fine_mine, 8), fine_mine), :] = fine_half[...]
+    down_out[pl.ds(pl.multiple_of(core * down_len, 8), down_len), :] = down_half[...]
+    mix_swap.wait()
+    mix_total[...] = mix_total[...] + mix_peer[...]
+    mixing_out[...] = mix_total[pl.ds(me, 1), 0:n]
+    down_swap.wait()
+    down_out[pl.ds(pl.multiple_of(other * down_len, 8), down_len), :] = down_half_peer[...]
+    fine_swap.wait()
+    fine_out[pl.ds(pl.multiple_of(other * fine_mine, 8), fine_mine), :] = fine_half_peer[...]
+
+
+def fused_fits(mesh, features, w_down):
+    n = mesh.shape["space"]
+    batch, ny, ex, ez, ch = features.shape
+    cc = w_down.shape[2]
+    spots = ex * ez // 4
+    return (
+        batch == mesh.shape["groups"] * mesh.shape["sample"]
+        and ny == 2 * n
+        and mesh.shape["sample"] == 2
+        and n % 8 == 0
+        and ch == 128
+        and cc % 128 == 0
+        and ez % 16 == 0
+        and ex % 2 == 0
+        and spots % 8 == 0
+        and (spots * cc) % (n * 128 * 16) == 0
+        and (27 * ch) % (n * 16) == 0
+        and (8 * ch) % (n * 32) == 0
+    )
+
+
+def fused(mesh, features, w_fine, w_down, mixing, cotangent):
+    n = lax.axis_size("space")
+    _, _, ex, ez, ch = features.shape
+    cc = w_down.shape[2]
+    batch = lax.axis_size("sample")
+    scale = float(batch * 2 * n * ex * ez) ** (-0.5)
+    plane, spots, lanes = ex * ez, ex * ez // 4, 128
+    rows = spots * cc // lanes // n
+    fine_rows, down_rows = 27 * ch // n, 8 * ch // n
+    half = fine_rows // 2
+    part = -(-half // 16) * 16
+    down_part = down_rows // 2
+    down_len = down_part * cc // lanes
+    vm = pltpu.VMEM
+    dma = pltpu.SemaphoreType.DMA
+    scratch = [
+        vm((2, ex, ez, ch), BF16), vm((2, ex, ez, ch), BF16), vm((2, ex, ez, ch), BF16),
+        vm((2, ex, ez + 16, ch), F32),
+        vm((4, ex + 2, ez, 3 * ch), BF16), vm((4, ex + 2, ez, 3 * ch), BF16),
+        vm((3, 3 * ch, 4 * plane), BF16),
+        vm((plane, 2 * ch), F32),
+        vm((2, ex // 2, 2, ez, ch), F32),
+        vm((spots, 8 * ch), BF16), vm((8 * ch, spots), BF16),
+        vm((n * rows, lanes), F32),
+        vm((n, rows, lanes), BF16), vm((n, rows, lanes), BF16),
+        vm((n, rows, lanes), BF16), vm((n, rows, lanes), BF16),
+        vm((2, ex // 2, 2, ez, ch), F32),
+        vm((27 * ch, ch), BF16),
+        vm((n, part, ch), BF16), vm((n, part, ch), BF16), vm((n, part, ch), BF16),
+        vm((n, down_rows, cc), BF16),
+        vm((n, down_part, cc), BF16), vm((n, down_part, cc), BF16), vm((n, down_part, cc), BF16),
+        vm((n, lanes), F32), vm((n, n, lanes), F32), vm((n, lanes), F32), vm((n, lanes), F32),
+        vm((half, ch), F32), vm((half, ch), F32),
+        vm((down_len, lanes), F32), vm((down_len, lanes), F32),
+        dma((2,)), dma((2,)), dma((n - 1,)), dma((n - 1,)), dma((n - 1,)), dma((n - 1,)),
+        dma((n - 1,)), dma((n - 1,)),
+        dma((2,)), dma((2,)), dma((n,)), dma((n,)), dma, dma,
+        dma((n - 1,)), dma((n - 1,)), dma((n - 1,)), dma((n - 1,)), dma((3,)), dma((3,)),
+    ]
+    spec = pl.BlockSpec(memory_space=pltpu.VMEM)
+    shapes = (
+        jax.ShapeDtypeStruct(cotangent.shape, BF16),
+        jax.ShapeDtypeStruct(features.shape, BF16),
+        jax.ShapeDtypeStruct((fine_rows, ch), F32),
+        jax.ShapeDtypeStruct((down_rows * cc // lanes, lanes), F32),
+        jax.ShapeDtypeStruct((1, n), F32),
+    )
+    a, b, c, d, e = pl.pallas_call(
+        functools.partial(fused_body, (n, ex, ez, ch, cc, scale)),
+        out_shape=shapes,
+        in_specs=[spec] * 5,
+        out_specs=tuple([spec] * 5),
+        scratch_shapes=scratch,
+        compiler_params=pltpu.CompilerParams(
+            collective_id=0, has_side_effects=True, vmem_limit_bytes=50 * 1024 * 1024
+        ),
+    )(features, w_fine, w_down, mixing, cotangent)
+    return a, b, c.reshape(-1), d.reshape(-1), e
 
 
 def with_halo(array, sides, width):
@@ -178,16 +576,19 @@
         P(),
         P(("groups", "sample"), None, "space"),
     )
-    return jax.shard_map(
-        local,
-        mesh=mesh,
-        in_specs=placed,
-        out_specs=(
-            P(("groups", "sample"), None, "space"),
-            P(("groups", "sample"), "space", None, None, None),
-            P(("groups", "space")),
-            P(("groups", "space")),
-            P(("groups", "space"), None),
-        ),
-        check_vma=False,
-    )
+    out_specs = (
+        P(("groups", "sample"), None, "space"),
+        P(("groups", "sample"), "space", None, None, None),
+        P(("groups", "space")),
+        P(("groups", "space")),
+        P(("groups", "space"), None),
+    )
+
+    def step(features, w_fine, w_down, mixing, cotangent):
+        kernel = functools.partial(fused, mesh) if fused_fits(mesh, features, w_down) else local
+        mapped = jax.shard_map(
+            kernel, mesh=mesh, in_specs=placed, out_specs=out_specs, check_vma=False
+        )
+        return mapped(features, w_fine, w_down, mixing, cotangent)
+
+    return step

time: 503 us -> 47.3 us (0.09)
  the two profiles are of different devices: /device:TPU:0 before, /device:TPU:11 now
where the time goes in v1:
time: 47.3 us; the launch traced here: 47 us
  Pallas kernels  38.7 us (82%)
  local copies, waits for them, and re-layouts  7.69 us (16%)
  between operations  0.66 us (1%)
    pallas_call x1, Pallas kernels, fused(): pl.pallas_call(functools.partial(fused_body, (n, ex, ez, ch, cc, scale)),...  38.7 us
    unnamed x15, local copies, waits for them, and re-layouts  7.69 us

profile of v1, /device:TPU:11, one launch (start us, length us, event | category | flops | bytes accessed | tf_op | source)
XLA Modules:
  0.0 47.0 jit_solution(15317238855072093851)
XLA Ops:
  0.6 0.0 copy-start
  0.6 1.2 %copy-done = bf16[27,128,128]{2,1,0:T(8,128)(2,1)S(1)} copy-done((bf16[27,128,128]{2,1,0:T(8,128)(2,1)S(1)}, bf16[27,128,128]{2,1,0:T(8,128)(2,1)}, u32[]{:S(2)}) %copy-start) | copy-done | bytes 884760
  1.8 0.0 copy-start.1
  1.8 1.0 %copy-done.1 = bf16[8,128,256]{2,1,0:T(8,128)(2,1)S(1)} copy-done((bf16[8,128,256]{2,1,0:T(8,128)(2,1)S(1)}, bf16[8,128,256]{2,1,0:T(8,128)(2,1)}, u32[]{:S(2)}) %copy-start.1) | copy-done | bytes 524312
  2.8 0.0 copy-start.2
  2.8 0.9 %copy-done.2 = bf16[1,2,16,16,128]{4,3,2,1,0:T(8,128)(2,1)S(1)} copy-done((bf16[1,2,16,16,128]{4,3,2,1,0:T(8,128)(2,1)S(1)}, bf16[1,2,16,16,128]{4,3,2,1,0:T(8,128)(2,1)}, u32[]{:S(2)}) %copy-start.2) | copy-done | bytes 131096
  3.7 0.0 copy-start.3
  3.8 0.8 %copy-done.3 = bf16[1,8,2048]{2,1,0:T(8,128)(2,1)S(1)} copy-done((bf16[1,8,2048]{2,1,0:T(8,128)(2,1)S(1)}, bf16[1,8,2048]{2,1,0:T(8,128)(2,1)}, u32[]{:S(2)}) %copy-start.3) | copy-done | bytes 32792
  4.5 0.0 copy-start.4
  4.5 0.7 %copy-done.4 = bf16[8,8]{1,0:T(8,128)(2,1)S(1)} copy-done((bf16[8,8]{1,0:T(8,128)(2,1)S(1)}, bf16[8,8]{1,0:T(8,128)(2,1)}, u32[]{:S(2)}) %copy-start.4) | copy-done | bytes 152
  5.2 38.7 %shard_map.92 = (bf16[1,8,2048]{2,1,0:T(8,128)(2,1)S(1)}, bf16[1,2,16,16,128]{4,3,2,1,0:T(8,128)(2,1)S(1)}, f32[432,128]{1,0:T(8,128)S(1)}, f32[256,128]{1,0:T(8,128)S(1)}, f32[1,8]{1,0:T(1,128)S(1)}) custom-call(bf16[1,2,16,16,128]{4,3,2,1,0:T(8,128)(2,1)S(1)} %copy-done.2, bf16[27,128,128]{2,1,0:T(8,128)(2,1)S(1)} %copy-done, ...), custom_call_target="tpu_custom_call" | custom-call | tf_op jit(solution)/shard_map/pallas_call | solution.py:392
  43.9 0.6 %copy.15 = bf16[1,8,2048]{2,1,0:T(8,128)(2,1)} copy(bf16[1,8,2048]{2,1,0:T(8,128)(2,1)S(1)} %get-tuple-element.20) | data formatting | bytes 65536
  44.5 0.7 %copy.16 = bf16[1,2,16,16,128]{4,3,2,1,0:T(8,128)(2,1)} copy(bf16[1,2,16,16,128]{4,3,2,1,0:T(8,128)(2,1)S(1)} %get-tuple-element.21) | data formatting | bytes 262144
  45.2 0.7 %copy.17 = f32[55296]{0:T(1024)} copy(f32[55296]{0:T(1024)S(1)} %bitcast.2) | data formatting | bytes 442368
  45.9 0.7 %copy.18 = f32[32768]{0:T(1024)} copy(f32[32768]{0:T(1024)S(1)} %bitcast.3) | data formatting | bytes 262144
  46.5 0.5 %copy.19 = f32[1,8]{1,0:T(1,128)} copy(f32[1,8]{1,0:T(1,128)S(1)} %get-tuple-element.24) | data formatting | bytes 64
Async XLA Ops:
  0.6 1.2 %copy-start = (bf16[27,128,128]{2,1,0:T(8,128)(2,1)S(1)}, bf16[27,128,128]{2,1,0:T(8,128)(2,1)}, u32[]{:S(2)}) copy-start(bf16[27,128,128]{2,1,0:T(8,128)(2,1)} %w_fine.1) | copy-start | bytes 2654212
  1.8 1.0 %copy-start.1 = (bf16[8,128,256]{2,1,0:T(8,128)(2,1)S(1)}, bf16[8,128,256]{2,1,0:T(8,128)(2,1)}, u32[]{:S(2)}) copy-start(bf16[8,128,256]{2,1,0:T(8,128)(2,1)} %w_down.1) | copy-start | bytes 1572868
  2.8 0.9 %copy-start.2 = (bf16[1,2,16,16,128]{4,3,2,1,0:T(8,128)(2,1)S(1)}, bf16[1,2,16,16,128]{4,3,2,1,0:T(8,128)(2,1)}, u32[]{:S(2)}) copy-start(bf16[1,2,16,16,128]{4,3,2,1,0:T(8,128)(2,1)} %features.1) | copy-start | bytes 393220
  3.7 0.8 %copy-start.3 = (bf16[1,8,2048]{2,1,0:T(8,128)(2,1)S(1)}, bf16[1,8,2048]{2,1,0:T(8,128)(2,1)}, u32[]{:S(2)}) copy-start(bf16[1,8,2048]{2,1,0:T(8,128)(2,1)} %cotangent.1) | copy-start | bytes 98308
  4.5 0.7 %copy-start.4 = (bf16[8,8]{1,0:T(8,128)(2,1)S(1)}, bf16[8,8]{1,0:T(8,128)(2,1)}, u32[]{:S(2)}) copy-start(bf16[8,8]{1,0:T(8,128)(2,1)} %mixing.1) | copy-start | bytes 388

commit v2 on v1

--- a/solution.py
+++ b/solution.py
@@ -16,17 +16,18 @@
 
 def fused_body(
     cfg,
-    features, w_fine, w_down, mixing, cotangent,
+    features_in, w_fine_in, w_down_in, mixing_in, cotangent_in,
     bottleneck, feature_grad, fine_out, down_out, mixing_out,
+    features, w_fine, w_down, mixing, cotangent, load_s,
     x_halo, g_halo, grad16, pad, x3, g3, xt, act, hid, folded, folded_t,
     stage, fwd_send, fwd_recv, back_send, back_recv, hid_grad,
-    fine16, fine_peer, fine_send, fine_recv,
-    down16, down_peer, down_send, down_recv,
+    fine16, fine_peer, fine_pair, fine_met, fine_send, fine_recv,
+    down16, down_peer, down_pair, down_met, down_send, down_recv,
     mix_send, mix_recv, mix_total, mix_peer,
     fine_half, fine_half_peer, down_half, down_half_peer,
     halo_s, halo_r, fwd_s, fwd_r, back_s, back_r, mix_s, mix_r,
     ghalo_s, ghalo_r, peer_s, peer_r, dpeer_s, dpeer_r,
-    fine_s, fine_r, down_s, down_r, last_s, last_r,
+    pair_s, pair_r, dpair_s, dpair_r, fine_s, fine_r, down_s, down_r, last_s, last_r,
 ):
     n, ex, ez, ch, cc, scale = cfg
     plane = ex * ez
@@ -57,6 +58,30 @@
         )
 
     has_prev, has_next = me > 0, me < n - 1
+    groups = n // 2
+    group, side_of = me // 2, lax.rem(me, 2)
+    partner = me + 1 - 2 * side_of
+
+    barrier = pltpu.get_barrier_semaphore()
+    for k in range(1, n):
+        pl.semaphore_signal(
+            barrier, inc=1, device_id={"space": lax.rem(me + k, n)}, device_id_type=MESH
+        )
+    pl.semaphore_signal(barrier, inc=1, device_id={"sample": other}, device_id_type=MESH)
+    loads = [
+        pltpu.make_async_copy(source, dest, load_s.at[i])
+        for i, (source, dest) in enumerate(
+            (
+                (features_in, features),
+                (w_fine_in, w_fine),
+                (w_down_in, w_down),
+                (mixing_in, mixing),
+                (cotangent_in, cotangent),
+            )
+        )
+    ]
+    for load in loads:
+        load.start()
 
     @pl.when(me == 0)
     def _():
@@ -68,14 +93,6 @@
         x_halo[1] = jnp.zeros(x_halo.shape[1:], BF16)
         g_halo[1] = jnp.zeros(g_halo.shape[1:], BF16)
 
-    barrier = pltpu.get_barrier_semaphore()
-    for k in range(1, n):
-        pl.semaphore_signal(
-            barrier, inc=1, device_id={"space": lax.rem(me + k, n)}, device_id_type=MESH
-        )
-    pl.semaphore_signal(barrier, inc=1, device_id={"sample": other}, device_id_type=MESH)
-    pl.semaphore_wait(barrier, n)
-
     def halo_copies(first, last, halo, send, recv):
         down = to_space(first, halo.at[1], send.at[0], recv.at[1], me - 1)
         up = to_space(last, halo.at[0], send.at[1], recv.at[0], me + 1)
@@ -96,9 +113,6 @@
 
         pl.when(has_prev)(with_prev)
         pl.when(has_next)(with_next)
-
-    x_copies = halo_copies(features.at[0, 0], features.at[0, 1], x_halo, halo_s, halo_r)
-    start_halo(x_copies)
 
     pad[:, :, 0:8, :] = jnp.zeros((2, ex, 8, ch), F32)
     pad[:, :, 8 + ez : 16 + ez, :] = jnp.zeros((2, ex, 8, ch), F32)
@@ -122,15 +136,23 @@
     def mm(a, b):
         return jnp.dot(a, b, preferred_element_type=F32)
 
+    loads[0].wait()
     spread_rows(x3, 1, features[0, 0], 0)
     spread_rows(x3, 2, features[0, 1], 1)
+    loads[1].wait()
     total = None
+    x_copies = halo_copies(features.at[0, 0], features.at[0, 1], x_halo, halo_s, halo_r)
     for sx in range(3):
         term = mm(window(x3, 1, sx), jnp.concatenate([taps(1, sx), taps(0, sx)], axis=1))
         total = term if total is None else total + term
         total = total + mm(
             window(x3, 2, sx), jnp.concatenate([taps(2, sx), taps(1, sx)], axis=1)
         )
+        if sx == 0:
+            act[...] = total
+            pl.semaphore_wait(barrier, n)
+            start_halo(x_copies)
+            total = act[...]
     act[...] = total
     wait_halo(x_copies)
     spread_rows(x3, 0, x_halo[0], 0)
@@ -147,6 +169,7 @@
         i, j, k = t // 4, t // 2 % 2, t % 2
         piece = hid[i, :, j, pl.ds(k, hz, stride=2), :].reshape(hx * hz, ch)
         folded[:, t * ch : (t + 1) * ch] = piece.astype(BF16)
+    loads[2].wait()
     coarse = mm(folded[...], w_down[...].reshape(8 * ch, cc)).astype(BF16).astype(F32)
     for h in range(halves):
         stage[pl.ds(h, hx * hz, stride=halves), :] = coarse[:, h * lanes : (h + 1) * lanes]
@@ -164,6 +187,8 @@
     coarse_copies = exchange(lambda who: fwd_send.at[who], fwd_recv, fwd_s, fwd_r)
     fwd_recv[me] = fwd_send[me]
 
+    loads[3].wait()
+    loads[4].wait()
     folded_t[...] = folded[...].T
     for sx in range(3):
         for j in range(4):
@@ -192,6 +217,9 @@
     mix_send[:, 0:n] = term
     mix_copies = exchange(lambda who: mix_send, mix_recv, mix_s, mix_r)
     mix_recv[me] = mix_send[...]
+    value = act[...]
+    sig = jax.nn.sigmoid(value)
+    act[...] = sig * (1.0 + value * (1.0 - sig))
 
     for copy in back_copies:
         copy.wait()
@@ -205,10 +233,7 @@
         piece = lax.dot_general(flat, w_down[t], CONTRACT_LAST, preferred_element_type=F32)
         hid_grad[i, :, j, pl.ds(k, hz, stride=2), :] = piece.reshape(hx, hz, ch)
     for side in range(2):
-        value = act[:, side * ch : (side + 1) * ch]
-        sig = jax.nn.sigmoid(value)
-        slope = sig * (1.0 + value * (1.0 - sig))
-        grad = hid_grad[side].reshape(plane, ch) * slope
+        grad = hid_grad[side].reshape(plane, ch) * act[:, side * ch : (side + 1) * ch]
         grad16[side] = grad.astype(BF16).reshape(ex, ez, ch)
     g_copies = halo_copies(grad16.at[0], grad16.at[1], g_halo, ghalo_s, ghalo_r)
     start_halo(g_copies)
@@ -219,6 +244,21 @@
         down_peer, dpeer_s, dpeer_r,
     )
     dpeer.start()
+
+    def down_mine(who):
+        rows_of = pl.ds(pl.multiple_of(core * down_part, 16), down_part)
+        return down16[who, rows_of, :].astype(F32) + down_peer[who].astype(F32)
+
+    def leave(met, outgoing, incoming, send, recv, k, to):
+        if k == groups - 1:
+            incoming[group] = met
+            return []
+        outgoing[k] = met
+        copy = to_space(
+            outgoing.at[k], incoming.at[group], send.at[k], recv.at[k], 2 * to + side_of
+        )
+        copy.start()
+        return [copy]
 
     flat_grad = grad16[...].reshape(2 * plane, ch)
     peer_copies = []
@@ -237,29 +277,41 @@
             copy.start()
             peer_copies.append(copy)
             done += 1
-        if t == 3:
+        if t == 1:
             dpeer.wait()
-            mine = down16[:, pl.ds(pl.multiple_of(core * down_part, 16), down_part), :]
-            down_send[...] = (mine.astype(F32) + down_peer[...].astype(F32)).astype(BF16)
-            down_copies = exchange(lambda who: down_send.at[who], down_recv, down_s, down_r)
-            down_recv[me] = down_send[me]
-
-    fine_copies = []
+            for g in range(groups):
+                down_pair[g] = down_mine(2 * g + 1 - side_of).astype(BF16)
+            dpair = to_space(down_pair, down_met, dpair_s, dpair_r, partner)
+            dpair.start()
+        if t == 5:
+            dpair.wait()
+            for k in range(groups):
+                to = lax.rem(group + 1 + k, groups)
+                met = (down_mine(2 * to + side_of) + down_met[to].astype(F32)).astype(BF16)
+                down_copies += leave(met, down_send, down_recv, down_s, down_r, k, to)
+
     for copy in peer_copies:
         copy.wait()
-    for k in range(1, n + 1):
-        who = lax.rem(me + k, n)
+
+    def fine_own(who):
         start = pl.multiple_of(who * fine_rows + core * fine_step, 16)
-        mine = fine16[pl.ds(start, part), :].astype(F32) + fine_peer[who].astype(F32)
-        if k < n:
-            fine_send[who] = mine.astype(BF16)
-            copy = to_space(
-                fine_send.at[who], fine_recv.at[me], fine_s.at[k - 1], fine_r.at[k - 1], who
-            )
-            copy.start()
-            fine_copies.append(copy)
-        else:
-            fine_recv[me] = mine.astype(BF16)
+        return fine16[pl.ds(start, part), :].astype(F32) + fine_peer[who].astype(F32)
+
+    pair_copies = []
+    for k in range(groups):
+        to = lax.rem(group + 1 + k, groups)
+        fine_pair[to] = fine_own(2 * to + 1 - side_of).astype(BF16)
+        copy = to_space(fine_pair.at[to], fine_met.at[to], pair_s.at[k], pair_r.at[k], partner)
+        copy.start()
+        pair_copies.append(copy)
+
+    fine_copies = []
+
+    def pass_on(k):
+        to = lax.rem(group + 1 + k, groups)
+        pair_copies[k].wait()
+        met = (fine_own(2 * to + side_of) + fine_met[to].astype(F32)).astype(BF16)
+        fine_copies.extend(leave(met, fine_send, fine_recv, fine_s, fine_r, k, to))
 
     def turned(i, sx):
         first = i * 9 + sx * 3
@@ -277,7 +329,13 @@
         total = total + mt(
             window(g3, 2, 2 - sx), jnp.concatenate([turned(0, sx), turned(1, sx)], axis=0)
         )
+        if sx == 1:
+            act[...] = total
+            pass_on(0)
+            total = act[...]
     act[...] = total
+    for k in range(1, groups - 2):
+        pass_on(k)
     wait_halo(g_copies)
     spread_rows(g3, 0, g_halo[0], 0)
     spread_rows(g3, 3, g_halo[1], 1)
@@ -286,6 +344,7 @@
         for sx in range(3):
             total = total + mt(window(g3, 3 * side, 2 - sx), turned(2 - 2 * side, sx))
         feature_grad[0, side] = total.astype(BF16).reshape(ex, ez, ch)
+        pass_on(groups - 2 + side)
 
     for copy in mix_copies:
         copy.wait()
@@ -295,7 +354,7 @@
 
     for copy in down_copies:
         copy.wait()
-    value = sum(down_recv[s].astype(F32) for s in range(n)) * scale
+    value = sum(down_recv[s].astype(F32) for s in range(groups)) * scale
     for h in range(halves):
         down_half[pl.ds(h, down_part, stride=halves), :] = value[:, h * lanes : (h + 1) * lanes]
     down_swap = to_peer(down_half, down_half_peer, last_s.at[1], last_r.at[1])
@@ -303,7 +362,7 @@
 
     for copy in fine_copies:
         copy.wait()
-    value = sum(fine_recv[s].astype(F32) for s in range(n)) * scale
+    value = sum(fine_recv[s].astype(F32) for s in range(groups)) * scale
     begin = fine_mine - fine_step
     fine_half[...] = jnp.where(core == 0, value[0:fine_mine], value[begin : begin + fine_mine])
     fine_swap = to_peer(fine_half, fine_half_peer, last_s.at[2], last_r.at[2])
@@ -319,6 +378,18 @@
     down_out[pl.ds(pl.multiple_of(other * down_len, 8), down_len), :] = down_half_peer[...]
     fine_swap.wait()
     fine_out[pl.ds(pl.multiple_of(other * fine_mine, 8), fine_mine), :] = fine_half_peer[...]
+
+
+def put_out(*refs):
+    sources, dests, done = refs[:5], refs[5:10], refs[10]
+    copies = [
+        pltpu.make_async_copy(source, dest, done.at[i])
+        for i, (source, dest) in enumerate(zip(sources, dests))
+    ]
+    for copy in copies:
+        copy.start()
+    for copy in copies:
+        copy.wait()
 
 
 def fused_fits(mesh, features, w_down):
@@ -357,7 +428,10 @@
     down_len = down_part * cc // lanes
     vm = pltpu.VMEM
     dma = pltpu.SemaphoreType.DMA
+    groups = n // 2
+    arrays = (features, w_fine, w_down, mixing, cotangent)
     scratch = [
+        *[vm(array.shape, BF16) for array in arrays], dma((5,)),
         vm((2, ex, ez, ch), BF16), vm((2, ex, ez, ch), BF16), vm((2, ex, ez, ch), BF16),
         vm((2, ex, ez + 16, ch), F32),
         vm((4, ex + 2, ez, 3 * ch), BF16), vm((4, ex + 2, ez, 3 * ch), BF16),
@@ -370,18 +444,20 @@
         vm((n, rows, lanes), BF16), vm((n, rows, lanes), BF16),
         vm((2, ex // 2, 2, ez, ch), F32),
         vm((27 * ch, ch), BF16),
-        vm((n, part, ch), BF16), vm((n, part, ch), BF16), vm((n, part, ch), BF16),
+        vm((n, part, ch), BF16), *[vm((groups, part, ch), BF16)] * 4,
         vm((n, down_rows, cc), BF16),
-        vm((n, down_part, cc), BF16), vm((n, down_part, cc), BF16), vm((n, down_part, cc), BF16),
+        vm((n, down_part, cc), BF16), *[vm((groups, down_part, cc), BF16)] * 4,
         vm((n, lanes), F32), vm((n, n, lanes), F32), vm((n, lanes), F32), vm((n, lanes), F32),
         vm((half, ch), F32), vm((half, ch), F32),
         vm((down_len, lanes), F32), vm((down_len, lanes), F32),
         dma((2,)), dma((2,)), dma((n - 1,)), dma((n - 1,)), dma((n - 1,)), dma((n - 1,)),
         dma((n - 1,)), dma((n - 1,)),
         dma((2,)), dma((2,)), dma((n,)), dma((n,)), dma, dma,
-        dma((n - 1,)), dma((n - 1,)), dma((n - 1,)), dma((n - 1,)), dma((3,)), dma((3,)),
+        dma((groups,)), dma((groups,)), dma, dma,
+        *[dma((groups - 1,))] * 4, dma((3,)), dma((3,)),
     ]
     spec = pl.BlockSpec(memory_space=pltpu.VMEM)
+    far = pl.BlockSpec(memory_space=pltpu.HBM)
     shapes = (
         jax.ShapeDtypeStruct(cotangent.shape, BF16),
         jax.ShapeDtypeStruct(features.shape, BF16),
@@ -389,16 +465,24 @@
         jax.ShapeDtypeStruct((down_rows * cc // lanes, lanes), F32),
         jax.ShapeDtypeStruct((1, n), F32),
     )
-    a, b, c, d, e = pl.pallas_call(
+    results = pl.pallas_call(
         functools.partial(fused_body, (n, ex, ez, ch, cc, scale)),
         out_shape=shapes,
-        in_specs=[spec] * 5,
+        in_specs=[far] * 5,
         out_specs=tuple([spec] * 5),
         scratch_shapes=scratch,
         compiler_params=pltpu.CompilerParams(
-            collective_id=0, has_side_effects=True, vmem_limit_bytes=50 * 1024 * 1024
+            collective_id=0, has_side_effects=True, vmem_limit_bytes=65472 * 1024
         ),
-    )(features, w_fine, w_down, mixing, cotangent)
+    )(*arrays)
+    a, b, c, d, e = pl.pallas_call(
+        put_out,
+        out_shape=shapes,
+        in_specs=[spec] * 5,
+        out_specs=tuple([far] * 5),
+        scratch_shapes=[dma((5,))],
+        compiler_params=pltpu.CompilerParams(vmem_limit_bytes=65472 * 1024),
+    )(*results)
     return a, b, c.reshape(-1), d.reshape(-1), e
 
 

time: 47.3 us -> 43.7 us (0.924)
  the two profiles are of different devices: /device:TPU:11 before, /device:TPU:0 now
where the time goes in v2:
time: 43.7 us; the launch traced here: 43.6 us
  Pallas kernels  42.9 us (98%)
  between operations  0.64 us (1%)
    pallas_call x1, Pallas kernels, fused(): pl.pallas_call(functools.partial(fused_body, (n, ex, ez, ch, cc, scale)),...  41 us
    pallas_call x1, Pallas kernels, fused(): pl.pallas_call(put_out, out_shape=shapes, in_specs=[spec] * 5, out_specs=...  1.91 us

profile of v2, /device:TPU:0, one launch (start us, length us, event | category | flops | bytes accessed | tf_op | source)
XLA Modules:
  0.0 43.6 jit_solution(16375472320665759339)
XLA Ops:
  0.6 41.0 %shard_map.92 = (bf16[1,8,2048]{2,1,0:T(8,128)(2,1)}, bf16[1,2,16,16,128]{4,3,2,1,0:T(8,128)(2,1)}, f32[432,128]{1,0:T(8,128)}, f32[256,128]{1,0:T(8,128)}, f32[1,8]{1,0:T(1,128)}) custom-call(bf16[1,2,16,16,128]{4,3,2,1,0:T(8,128)(2,1)} %features_in.1, bf16[27,128,128]{2,1,0:T(8,128)(2,1)} %w_fine_in.1, bf16[8,128,256]{2,1,0:T(8,128)(2,1)} %w_down_in.1, ...), custom_call_target="tpu_custom_call" | custom-call | tf_op jit(solution)/shard_map/pallas_call | solution.py:468
  41.6 1.9 %shard_map.93 = (bf16[1,8,2048]{2,1,0:T(8,128)(2,1)}, bf16[1,2,16,16,128]{4,3,2,1,0:T(8,128)(2,1)}, f32[432,128]{1,0:T(8,128)}, f32[256,128]{1,0:T(8,128)}, f32[1,8]{1,0:T(1,128)}) custom-call(bf16[1,8,2048]{2,1,0:T(8,128)(2,1)} %get-tuple-element.15.refs_0_, bf16[1,2,16,16,128]{4,3,2,1,0:T(8,128)(2,1)} %get-tuple-element.16.refs_1_, ...), custom_call_target="tpu_custom_call" | custom-call | tf_op jit(solution)/shard_map/pallas_call | solution.py:478

commit v3 on v2

--- a/solution.py
+++ b/solution.py
@@ -236,7 +236,6 @@
         grad = hid_grad[side].reshape(plane, ch) * act[:, side * ch : (side + 1) * ch]
         grad16[side] = grad.astype(BF16).reshape(ex, ez, ch)
     g_copies = halo_copies(grad16.at[0], grad16.at[1], g_halo, ghalo_s, ghalo_r)
-    start_halo(g_copies)
 
     down16[...] = mm(folded_t[...], flat).astype(BF16).reshape(n, down_rows, cc)
     dpeer = to_peer(
@@ -277,18 +276,15 @@
             copy.start()
             peer_copies.append(copy)
             done += 1
-        if t == 1:
-            dpeer.wait()
-            for g in range(groups):
-                down_pair[g] = down_mine(2 * g + 1 - side_of).astype(BF16)
-            dpair = to_space(down_pair, down_met, dpair_s, dpair_r, partner)
-            dpair.start()
-        if t == 5:
-            dpair.wait()
-            for k in range(groups):
-                to = lax.rem(group + 1 + k, groups)
-                met = (down_mine(2 * to + side_of) + down_met[to].astype(F32)).astype(BF16)
-                down_copies += leave(met, down_send, down_recv, down_s, down_r, k, to)
+
+    dpeer.wait()
+    dpair_copies = []
+    for k in range(groups):
+        to = lax.rem(group + 1 + k, groups)
+        down_pair[to] = down_mine(2 * to + 1 - side_of).astype(BF16)
+        copy = to_space(down_pair.at[to], down_met.at[to], dpair_s.at[k], dpair_r.at[k], partner)
+        copy.start()
+        dpair_copies.append(copy)
 
     for copy in peer_copies:
         copy.wait()
@@ -304,6 +300,13 @@
         copy = to_space(fine_pair.at[to], fine_met.at[to], pair_s.at[k], pair_r.at[k], partner)
         copy.start()
         pair_copies.append(copy)
+    start_halo(g_copies)
+
+    for k in range(groups):
+        to = lax.rem(group + 1 + k, groups)
+        dpair_copies[k].wait()
+        met = (down_mine(2 * to + side_of) + down_met[to].astype(F32)).astype(BF16)
+        down_copies += leave(met, down_send, down_recv, down_s, down_r, k, to)
 
     fine_copies = []
 
@@ -453,7 +456,7 @@
         dma((2,)), dma((2,)), dma((n - 1,)), dma((n - 1,)), dma((n - 1,)), dma((n - 1,)),
         dma((n - 1,)), dma((n - 1,)),
         dma((2,)), dma((2,)), dma((n,)), dma((n,)), dma, dma,
-        dma((groups,)), dma((groups,)), dma, dma,
+        *[dma((groups,))] * 4,
         *[dma((groups - 1,))] * 4, dma((3,)), dma((3,)),
     ]
     spec = pl.BlockSpec(memory_space=pltpu.VMEM)

time: 43.7 us -> 43 us (0.984)
  Pallas kernels: 42.9 us -> 42.2 us
    pallas_call x1, Pallas kernels: 41 us -> 40.3 us  [fused(): pl.pallas_call(functools.partial(fused_body, (n, ex, ez, ch, cc, scale)),...]
where the time goes in v3:
time: 43 us; the launch traced here: 42.8 us
  Pallas kernels  42.2 us (98%)
  between operations  0.64 us (1%)
    pallas_call x1, Pallas kernels, fused(): pl.pallas_call(functools.partial(fused_body, (n, ex, ez, ch, cc, scale)),...  40.3 us
    pallas_call x1, Pallas kernels, fused(): pl.pallas_call(put_out, out_shape=shapes, in_specs=[spec] * 5, out_specs=...  1.91 us

profile of v3, /device:TPU:0, one launch (start us, length us, event | category | flops | bytes accessed | tf_op | source)
XLA Modules:
  0.0 42.8 jit_solution(14116982616772823173)
XLA Ops:
  0.6 40.3 %shard_map.92 = (bf16[1,8,2048]{2,1,0:T(8,128)(2,1)}, bf16[1,2,16,16,128]{4,3,2,1,0:T(8,128)(2,1)}, f32[432,128]{1,0:T(8,128)}, f32[256,128]{1,0:T(8,128)}, f32[1,8]{1,0:T(1,128)}) custom-call(bf16[1,2,16,16,128]{4,3,2,1,0:T(8,128)(2,1)} %features_in.1, bf16[27,128,128]{2,1,0:T(8,128)(2,1)} %w_fine_in.1, bf16[8,128,256]{2,1,0:T(8,128)(2,1)} %w_down_in.1, ...), custom_call_target="tpu_custom_call" | custom-call | tf_op jit(solution)/shard_map/pallas_call | solution.py:471
  40.9 1.9 %shard_map.93 = (bf16[1,8,2048]{2,1,0:T(8,128)(2,1)}, bf16[1,2,16,16,128]{4,3,2,1,0:T(8,128)(2,1)}, f32[432,128]{1,0:T(8,128)}, f32[256,128]{1,0:T(8,128)}, f32[1,8]{1,0:T(1,128)}) custom-call(bf16[1,8,2048]{2,1,0:T(8,128)(2,1)} %get-tuple-element.15.refs_0_, bf16[1,2,16,16,128]{4,3,2,1,0:T(8,128)(2,1)} %get-tuple-element.16.refs_1_, ...), custom_call_target="tpu_custom_call" | custom-call | tf_op jit(solution)/shard_map/pallas_call | solution.py:481
